TPU v7x, 256 devices: a whole 4x4x8 slice. The times are simulated.
256 devices in a mesh: row: 16 (over y, z_hi), col: 16 (over x, z_lo, core).
Axes of the slice: x: 4, y: 4, z: 8 (z_hi: 4, z_lo: 2; z = z_hi * 2 + z_lo), core: 2. Of those that a mesh axis runs over, the one named last changes fastest.
Arguments:
- fit_tiles: bfloat16 [32, 96, 128, 128], P('row', 'col'), may hold values from -6 to 6
- aux_list: int32 [32, 96], P('row', 'col'), may hold values from 0 to 11, as said below
- aux_count: int32 [32, 16], P('row', 'col'), may hold values from 1 to 6, as said below
- metric: bfloat16 [192, 128, 128], P('col', 'row'), may hold values from -0.5 to 0.5
Outputs:
- exchange: float32 [4096, 4096], P('col', 'row')
Inputs may be any that keep to these rules, and one draw needn't show every extreme that they name: `aux_list`: within one atom block and one col shard, the first 6 slots name distinct auxiliary blocks. `aux_count`: counts follow a density per atom block; the largest is reached in every draw.
All inputs are finite; a program needn't handle non-finite values.
Results may differ from a plain program's by a relative error of at most 0.0015.
Values may be sent and summed in bfloat16 or wider, within the bound.
No kernel may reach another device: no remote copies, remote signals or barrier semaphores. Data moves between devices by JAX's collectives and lax.ppermute only.
A program may use at most 64 MiB of HBM per device.

v0:
```python
import jax
import jax.numpy as jnp
from jax import lax
from jax.sharding import PartitionSpec as P

AUXB = 128
QS = 6


def expand(fitted, marked, local_aux):
    onehot = (marked[:, :, None] == jnp.arange(local_aux, dtype=jnp.int32)[None, None, :]).astype(
        jnp.bfloat16
    )
    dense = jnp.einsum("asq,asmn->amqn", onehot, fitted, preferred_element_type=jnp.float32).astype(
        jnp.bfloat16
    )
    return dense.reshape(fitted.shape[0] * fitted.shape[2], local_aux * fitted.shape[3])


def local(fit_tiles, aux_list, aux_count, metric):
    slots = fit_tiles.shape[1]
    local_aux = metric.shape[0]
    full_metric = lax.all_gather(metric, "row", axis=1, tiled=True)
    alive = jnp.arange(slots, dtype=jnp.int32)[None, :] < aux_count
    marked = jnp.where(alive, aux_list, local_aux)
    picked = full_metric[aux_list]
    fitted = jnp.einsum(
        "asmk,askn->asmn", fit_tiles, picked, preferred_element_type=jnp.float32
    ).astype(jnp.bfloat16)
    dense = expand(fitted, marked, local_aux)
    factor = 1.0 / (QS * lax.axis_size("col") * AUXB) ** 0.5
    gathered = lax.all_gather(dense, "row", axis=0, tiled=True)
    summed = lax.psum_scatter(
        jnp.dot(gathered, dense.T, preferred_element_type=jnp.float32),
        "col",
        scatter_dimension=0,
        tiled=True,
    )
    return summed * factor


def solution(mesh):
    placed = (P("row", "col", None, None), P("row", "col"), P("row", "col"), P("col", "row", None))
    return jax.shard_map(
        local, mesh=mesh, in_specs=placed, out_specs=P("col", "row"), check_vma=False
    )
```

profile of v0, /device:TPU:8, one launch (start us, length us, event | category | flops | bytes accessed | tf_op | source)
XLA Modules:
  0.0 312.3 jit_solution(8098111673905659290)
XLA Ops:
  6.5 0.0 copy-start
  6.5 0.0 all-gather.2.cloned.1.call-start
  6.5 0.8 compare_select_fusion.1
  7.3 0.1 reshape.7
  7.4 44.8 %all_gather.6 = bf16[12,128,128]{2,1,0:T(8,128)(2,1)S(1)} all-gather(bf16[12,8,128]{2,1,0:T(8,128)(2,1)} %param.7), channel_id=1, replica_groups=mesh['row'=16,'col'=16] {'row'}, dimensions={1}, use_global_device_ids=true | all-gather | bytes 417792 | tf_op jit(solution)/shard_map/all_gather | solution.py:23
  52.2 0.6 gather_fusion
  52.8 0.0 copy-done
  52.8 0.4 fusion.5
  53.3 0.3 copy.6
  53.6 0.6 convolution_convert_fusion
  54.1 0.2 copy.11
  54.3 1.2 copy.8
  55.6 0.0 all-gather.2.cloned.1.call-update
  55.6 0.0 reduce-scatter.2.cloned.1.call-start
  55.6 149.9 %all-gather.2.cloned.1.call-done = bf16[4096,1536]{0,1:T(8,128)(2,1)} async-done(((bf16[256,1536]{0,1:T(8,128)(2,1)}), bf16[4096,1536]{0,1:T(8,128)(2,1)}) %all-gather.2.cloned.1.call-update) | async-done | bytes 12582928 | tf_op jit(solution)/shard_map/all_gather | solution.py:32
  205.5 10.2 %fusion.6 = f32[4096,256]{1,0:T(8,128)} fusion(bf16[4096,1536]{0,1:T(8,128)(2,1)} %all-gather.2.cloned.1.call-done, bf16[256,1536]{1,0:T(8,128)(2,1)S(1)} %bitcast.22), kind=kOutput, calls=%fused_computation.13 | convolution fusion | flops 3221225472 | bytes 17563648 | tf_op jit(solution)/shard_map/dot_general | solution.py:34
  215.8 0.0 reduce-scatter.2.cloned.1.call-update
  215.8 88.0 %reduce-scatter.2.cloned.1.call-done = f32[256,256]{1,0:T(8,128)} async-done(((f32[4096,256]{1,0:T(8,128)}), f32[256,256]{1,0:T(8,128)}) %reduce-scatter.2.cloned.1.call-update) | async-done | bytes 262160 | tf_op jit(solution)/shard_map/reduce_scatter | solution.py:33
  303.8 1.7 broadcast_multiply_fusion
  (1 shorter events, 0.0 us)
Async XLA Ops:
  6.5 46.3 %copy-start = (bf16[2,6,128,128]{3,2,1,0:T(8,128)(2,1)S(1)}, bf16[2,6,128,128]{3,2,1,0:T(8,128)(2,1)}, u32[]{:S(2)}) copy-start(bf16[2,6,128,128]{3,2,1,0:T(8,128)(2,1)} %param.4) | copy-start | bytes 1179652
  6.5 199.0 %all-gather.2.cloned.1.call-start = ((), (), s32[]{:S(2)}) async-start(), calls=%async_computation.1 | async-start | bytes 13369344 | tf_op jit(solution)/shard_map/all_gather | solution.py:32
  55.6 248.2 %reduce-scatter.2.cloned.1.call-start = ((), (), s32[]{:S(2)}) async-start(), calls=%async_computation.2 | async-start | bytes 4456448 | tf_op jit(solution)/shard_map/reduce_scatter | solution.py:33
Sparse Core Ops, SparseCore 0:
  55.7 149.7 all-gather.1
  215.9 87.8 reduce-scatter.1
where the time goes:
time: 313 us; the launch traced here: 312 us
  waiting for transfers between devices  238 us (76%)
  blocking collectives  44.8 us (14%)
  between operations  13.4 us (4%)
  matrix products  11.2 us (4%)
    all_gather x1, waiting for transfers between devices, local(): gathered = lax.all_gather(dense, 'row', axis=0, tiled=True)  150 us
    reduce_scatter x1, waiting for transfers between devices, local(): lax.psum_scatter(jnp.dot(gathered, dense.T, preferred_element_type=jnp.fl...  88 us
    all_gather x1, blocking collectives, local(): full_metric = lax.all_gather(metric, 'row', axis=1, tiled=True)  44.8 us
    dot_general x1, matrix products, local(): jnp.dot(gathered, dense.T, preferred_element_type=jnp.float32)  10.2 us
  transfers between devices with their start and end apart: 2, of which 2 were waited for; matrix products, arithmetic and copies ran while one was open for 0% of the time, Pallas kernels for 0%

commit v1 on v0

--- a/solution.py
+++ b/solution.py
@@ -20,7 +20,9 @@
 def local(fit_tiles, aux_list, aux_count, metric):
     slots = fit_tiles.shape[1]
     local_aux = metric.shape[0]
-    full_metric = lax.all_gather(metric, "row", axis=1, tiled=True)
+    full_metric = jnp.concatenate(
+        lax.all_to_all(jnp.stack([metric] * lax.axis_size("row")), "row", 0, 0), axis=1
+    )
     alive = jnp.arange(slots, dtype=jnp.int32)[None, :] < aux_count
     marked = jnp.where(alive, aux_list, local_aux)
     picked = full_metric[aux_list]

time: 313 us -> 291 us (0.930)
  blocking collectives: 44.8 us -> 0 us
  starting transfers between devices: 0.04 us -> 11.6 us
  waiting for transfers between devices: 238 us -> 248 us
    all_gather x1 -> x0, blocking collectives: 44.8 us -> none  [local(): full_metric = lax.all_gather(metric, 'row', axis=1, tiled=True)]
    all_to_all x0 -> x1, waiting for transfers between devices: none -> 13 us  [local(): lax.all_to_all(jnp.stack([metric] * lax.axis_size('row')), 'row', 0, 0)]
    all_to_all x0 -> x1, starting transfers between devices: none -> 11.6 us  [local(): lax.all_to_all(jnp.stack([metric] * lax.axis_size('row')), 'row', 0, 0)]
  transfers between devices with their start and end apart: 2 -> 3, of which waited for: 2 -> 3; matrix products, arithmetic and copies ran while one was open for 0% -> 0% of each run, Pallas kernels for 0% -> 0%
where the time goes in v1:
time: 291 us
  waiting for transfers between devices  248 us (85%)
  between operations  13.5 us (5%)
  starting transfers between devices  11.6 us (4%)
  matrix products  11.2 us (4%)
  local copies, waits for them, and re-layouts  4.12 us (1%)
    all_gather x1, waiting for transfers between devices, local(): gathered = lax.all_gather(dense, 'row', axis=0, tiled=True)  147 us
    reduce_scatter x1, waiting for transfers between devices, local(): lax.psum_scatter(jnp.dot(gathered, dense.T, preferred_element_type=jnp.fl...  88.2 us
    all_to_all x1, waiting for transfers between devices, local(): lax.all_to_all(jnp.stack([metric] * lax.axis_size('row')), 'row', 0, 0)  13 us
    all_to_all x1, starting transfers between devices, local(): lax.all_to_all(jnp.stack([metric] * lax.axis_size('row')), 'row', 0, 0)  11.6 us
    dot_general x1, matrix products, local(): jnp.dot(gathered, dense.T, preferred_element_type=jnp.float32)  10.2 us
  transfers between devices with their start and end apart: 3, of which 3 were waited for; matrix products, arithmetic and copies ran while one was open for 0% of the time, Pallas kernels for 0%

profile of v1, /device:TPU:8, one launch (start us, length us, event | category | flops | bytes accessed | tf_op | source)
XLA Modules:
  0.0 291.0 jit_solution(8231469806074784128)
XLA Ops:
  6.5 0.0 copy-start
  6.5 1.6 stack.2
  8.1 11.6 %all-to-all-start = ((bf16[16,12,8,128]{3,2,1,0:T(8,128)(2,1)}), bf16[16,12,8,128]{3,2,1,0:T(8,128)(2,1)S(1)}, u32[]{:S(2)}, u32[]{:S(2)}) async-start(bf16[16,12,8,128]{3,2,1,0:T(8,128)(2,1)} %stack.2), calls=%async_computation | async-start | bytes 786432 | tf_op jit(solution)/shard_map/all_to_all | solution.py:24
  19.7 0.0 all-gather.2.cloned.1.call-start
  19.7 0.8 compare_select_fusion.1
  20.5 0.1 reshape.17
  20.6 13.0 %all-to-all-done = bf16[16,12,8,128]{3,2,1,0:T(8,128)(2,1)S(1)} async-done(((bf16[16,12,8,128]{3,2,1,0:T(8,128)(2,1)}), bf16[16,12,8,128]{3,2,1,0:T(8,128)(2,1)S(1)}, u32[]{:S(2)}, u32[]{:S(2)}) %all-to-all-start) | async-done | bytes 393248 | tf_op jit(solution)/shard_map/all_to_all | solution.py:24
  33.5 0.1 copy.17
  33.6 0.6 gather_fusion
  34.3 0.0 copy-done
  34.3 0.4 fusion
  34.7 0.3 copy.8
  35.0 0.5 convolution_convert_fusion
  35.6 0.2 copy.16
  35.8 1.2 copy.12
  37.0 0.0 all-gather.2.cloned.1.call-update
  37.0 0.0 reduce-scatter.2.cloned.1.call-start
  37.1 147.0 %all-gather.2.cloned.1.call-done = bf16[4096,1536]{0,1:T(8,128)(2,1)} async-done(((bf16[256,1536]{0,1:T(8,128)(2,1)}), bf16[4096,1536]{0,1:T(8,128)(2,1)}) %all-gather.2.cloned.1.call-update) | async-done | bytes 12582928 | tf_op jit(solution)/shard_map/all_gather | solution.py:34
  184.1 10.2 %fusion.4 = f32[4096,256]{1,0:T(8,128)} fusion(bf16[4096,1536]{0,1:T(8,128)(2,1)} %all-gather.2.cloned.1.call-done, bf16[256,1536]{1,0:T(8,128)(2,1)S(1)} %bitcast.27), kind=kOutput, calls=%fused_computation.13 | convolution fusion | flops 3221225472 | bytes 17563648 | tf_op jit(solution)/shard_map/dot_general | solution.py:36
  194.3 0.0 reduce-scatter.2.cloned.1.call-update
  194.3 88.2 %reduce-scatter.2.cloned.1.call-done = f32[256,256]{1,0:T(8,128)} async-done(((f32[4096,256]{1,0:T(8,128)}), f32[256,256]{1,0:T(8,128)}) %reduce-scatter.2.cloned.1.call-update) | async-done | bytes 262160 | tf_op jit(solution)/shard_map/reduce_scatter | solution.py:35
  282.5 1.7 broadcast_multiply_fusion
  (1 shorter events, 0.0 us)
Async XLA Ops:
  6.5 27.7 %copy-start = (bf16[2,6,128,128]{3,2,1,0:T(8,128)(2,1)S(1)}, bf16[2,6,128,128]{3,2,1,0:T(8,128)(2,1)}, u32[]{:S(2)}) copy-start(bf16[2,6,128,128]{3,2,1,0:T(8,128)(2,1)} %param.4) | copy-start | bytes 1179652
  8.1 25.4 %all-to-all-start = ((bf16[16,12,8,128]{3,2,1,0:T(8,128)(2,1)}), bf16[16,12,8,128]{3,2,1,0:T(8,128)(2,1)S(1)}, u32[]{:S(2)}, u32[]{:S(2)}) async-start(bf16[16,12,8,128]{3,2,1,0:T(8,128)(2,1)} %stack.2), calls=%async_computation | async-start | bytes 786432 | tf_op jit(solution)/shard_map/all_to_all | solution.py:24
  19.7 164.4 %all-gather.2.cloned.1.call-start = ((), (), s32[]{:S(2)}) async-start(), calls=%async_computation.2 | async-start | bytes 13369344 | tf_op jit(solution)/shard_map/all_gather | solution.py:34
  37.0 245.5 %reduce-scatter.2.cloned.1.call-start = ((), (), s32[]{:S(2)}) async-start(), calls=%async_computation.3 | async-start | bytes 4456448 | tf_op jit(solution)/shard_map/reduce_scatter | solution.py:35
Sparse Core Ops, SparseCore 0:
  37.1 146.9 all-gather.1
  194.4 87.9 reduce-scatter.1
